TPU v7x, 32 devices: a whole 2x2x4 slice. The times are simulated.
32 devices in a mesh: groups: 2 (over y), row: 4 (over z), col: 4 (over x, core).
Axes of the slice: x: 2, y: 2, z: 4, core: 2. Of those that a mesh axis runs over, the one named last changes fastest.
Arguments:
- block_tiles: bfloat16 [8, 4, 128, 128, 128], P(('groups', 'row'), 'col'), parts along dimension 0, may hold values from -0.125 to 0.125
- tile_row: int32 [8, 4, 128], P(('groups', 'row'), 'col'), parts along dimension 0, may hold values from 0 to 11, as said below
- tile_col: int32 [8, 4, 128], P(('groups', 'row'), 'col'), parts along dimension 0, may hold values from 0 to 11, as said below
- tile_count: int32 [8, 4], P(('groups', 'row'), 'col'), parts along dimension 0, may hold values from 1 to 128, as said below
- objective: float32 [12288], P(('groups', 'col')), parts along dimension 0, may hold values from -6 to 6
- upper_bound: float32 [12288], P(('groups', 'col')), parts along dimension 0, may hold values from 0.5 to 4
- power_caps: float32 [64, 6144], P('groups', 'row'), parts along dimension 0, may hold values from -6 to 6
- primal_start: float32 [64, 6144], P('groups', 'col'), parts along dimension 0, may hold values from 0 to 0.5
- dual_start: float32 [64, 6144], P('groups', 'row'), parts along dimension 0, may hold values from 0 to 1
Outputs:
- primal_final: float32 [64, 6144], P('groups', 'col'), parts along dimension 0
- dual_final: float32 [64, 6144], P('groups', 'row'), parts along dimension 0
There are 2 independent parts, one for each index of `groups`. A program takes and returns all parts, laid end to end along the dimension named above; each array names one. Nothing has to cross between parts.
Inputs may be any that keep to these rules, and one draw needn't show every extreme that they name: `tile_row`: constraint block of a slot, local to its row index. `tile_col`: variable block of a slot, local to its col index; the slots of one device name distinct pairs of (tile_row, tile_col). `tile_count`: some device of every draw has all 128 slots live; the busiest devices hold about three times the mean.
All inputs are finite; a program needn't handle non-finite values.
Results may differ from a plain program's by a relative error of at most 0.0011.
Values sent between devices are 32-bit elements; how exact they have to be, the bound alone decides.
A program may use at most 64 MiB of HBM per device.

v0:
```python
import jax
import jax.numpy as jnp
from jax import lax
from jax.sharding import PartitionSpec as P

ITERS = 6


PRIMAL_STEP = 0.5
DUAL_STEP = 0.2


def per_device(
    block_tiles,
    tile_row,
    tile_col,
    tile_count,
    objective,
    upper_bound,
    power_caps,
    primal_start,
    dual_start,
):
    local_tiles = block_tiles[0, 0]
    local_rows = tile_row[0, 0]
    local_cols = tile_col[0, 0]
    slot_total = local_tiles.shape[0]
    block_size = local_tiles.shape[1]
    scenarios = primal_start.shape[0]
    row_blocks = dual_start.shape[1] // block_size
    col_blocks = primal_start.shape[1] // block_size
    live_slots = (jnp.arange(slot_total, dtype=jnp.int32) < tile_count[0, 0]).astype(jnp.float32)
    onehot_col = (local_cols[:, None] == jnp.arange(col_blocks, dtype=jnp.int32)[None, :]).astype(
        jnp.float32
    )
    onehot_row = (local_rows[:, None] == jnp.arange(row_blocks, dtype=jnp.int32)[None, :]).astype(
        jnp.float32
    )
    primal = primal_start
    dual = dual_start
    for iteration in range(ITERS):
        dual_low = dual.astype(jnp.bfloat16)
        dual_three = dual_low.reshape(scenarios, row_blocks, block_size)
        adjoint_selected = dual_three[:, local_rows]
        adjoint_product = jnp.einsum(
            "stb,tbk->stk", adjoint_selected, local_tiles, preferred_element_type=jnp.float32
        )
        adjoint_product = adjoint_product * live_slots[None, :, None]
        adjoint_pieces = jnp.einsum(
            "stk,tj->sjk", adjoint_product, onehot_col, precision=lax.Precision.HIGHEST
        )
        partial_adj = adjoint_pieces.reshape(scenarios, col_blocks * block_size)
        adjoint = lax.psum(partial_adj, "row")
        primal_next = jnp.minimum(
            jnp.maximum(primal - PRIMAL_STEP * (objective[None, :] - adjoint), 0.0),
            upper_bound[None, :],
        )
        extrap = (2.0 * primal_next - primal).astype(jnp.bfloat16)
        primal_three = extrap.reshape(scenarios, col_blocks, block_size)
        selected = primal_three[:, local_cols]
        product = jnp.einsum(
            "stk,tbk->stb", selected, local_tiles, preferred_element_type=jnp.float32
        )
        product = product * live_slots[None, :, None]
        pieces = jnp.einsum("stb,tj->sjb", product, onehot_row, precision=lax.Precision.HIGHEST)
        partial_fwd = pieces.reshape(scenarios, row_blocks * block_size)
        forward = lax.psum(partial_fwd, "col")
        dual = jnp.maximum(dual + DUAL_STEP * (power_caps - forward), 0.0)
        primal = primal_next
    return (primal, dual)


def solution(mesh):
    return jax.shard_map(
        per_device,
        mesh=mesh,
        in_specs=(
            P(("groups", "row"), "col", None, None, None),
            P(("groups", "row"), "col", None),
            P(("groups", "row"), "col", None),
            P(("groups", "row"), "col"),
            P(("groups", "col")),
            P(("groups", "col")),
            P("groups", "row"),
            P("groups", "col"),
            P("groups", "row"),
        ),
        out_specs=(P("groups", "col"), P("groups", "row")),
        check_vma=False,
    )
```

profile of v0, /device:TPU:0, one launch (start us, length us, event | category | flops | bytes accessed | tf_op | source)
XLA Modules:
  0.0 521.3 jit_solution(1171947677480797568)
XLA Ops:
  10.3 3.4 fusion.22
  16.5 37.6 %all-reduce.13.cloned.1.call-done = f32[32,1536]{1,0:T(8,128)} async-done(((f32[32,1536]{1,0:T(8,128)}), f32[32,1536]{1,0:T(8,128)}) %all-reduce.13.cloned.1.call-update) | async-done | bytes 196624 | tf_op jit(solution)/shard_map/psum | solution.py:53
  55.8 4.5 fusion.20
  63.1 31.5 %all-reduce.15.cloned.1.call-done = f32[32,1536]{1,0:T(8,128)} async-done(((f32[32,1536]{1,0:T(8,128)}), f32[32,1536]{1,0:T(8,128)}) %all-reduce.15.cloned.1.call-update) | async-done | bytes 196624 | tf_op jit(solution)/shard_map/psum | solution.py:67
  96.3 3.4 fusion.18
  99.7 2.0 fusion.42
  102.7 34.8 %all-reduce.17.cloned.1.call-done = f32[32,1536]{1,0:T(8,128)} async-done(((f32[32,1536]{1,0:T(8,128)}), f32[32,1536]{1,0:T(8,128)}) %all-reduce.17.cloned.1.call-update) | async-done | bytes 196624 | tf_op jit(solution)/shard_map/psum | solution.py:53
  139.3 4.5 fusion.16
  143.7 2.0 fusion.40
  146.5 31.5 %all-reduce.19.cloned.1.call-done = f32[32,1536]{1,0:T(8,128)} async-done(((f32[32,1536]{1,0:T(8,128)}), f32[32,1536]{1,0:T(8,128)}) %all-reduce.19.cloned.1.call-update) | async-done | bytes 196624 | tf_op jit(solution)/shard_map/psum | solution.py:67
  179.8 3.4 fusion.14
  186.0 34.9 %all-reduce.21.cloned.1.call-done = f32[32,1536]{1,0:T(8,128)} async-done(((f32[32,1536]{1,0:T(8,128)}), f32[32,1536]{1,0:T(8,128)}) %all-reduce.21.cloned.1.call-update) | async-done | bytes 196624 | tf_op jit(solution)/shard_map/psum | solution.py:53
  222.7 4.5 fusion.12
  227.1 2.0 fusion.36
  230.1 31.3 %all-reduce.23.cloned.1.call-done = f32[32,1536]{1,0:T(8,128)} async-done(((f32[32,1536]{1,0:T(8,128)}), f32[32,1536]{1,0:T(8,128)}) %all-reduce.23.cloned.1.call-update) | async-done | bytes 196624 | tf_op jit(solution)/shard_map/psum | solution.py:67
  263.2 3.4 fusion.10
  266.6 2.0 fusion.34
  269.3 34.9 %all-reduce.25.cloned.1.call-done = f32[32,1536]{1,0:T(8,128)} async-done(((f32[32,1536]{1,0:T(8,128)}), f32[32,1536]{1,0:T(8,128)}) %all-reduce.25.cloned.1.call-update) | async-done | bytes 196624 | tf_op jit(solution)/shard_map/psum | solution.py:53
  306.1 4.5 fusion.8
  310.6 2.0 fusion.32
  313.4 31.5 %all-reduce.27.cloned.1.call-done = f32[32,1536]{1,0:T(8,128)} async-done(((f32[32,1536]{1,0:T(8,128)}), f32[32,1536]{1,0:T(8,128)}) %all-reduce.27.cloned.1.call-update) | async-done | bytes 196624 | tf_op jit(solution)/shard_map/psum | solution.py:67
  346.6 3.4 fusion.6
  350.0 2.0 fusion.30
  353.1 34.7 %all-reduce.29.cloned.1.call-done = f32[32,1536]{1,0:T(8,128)} async-done(((f32[32,1536]{1,0:T(8,128)}), f32[32,1536]{1,0:T(8,128)}) %all-reduce.29.cloned.1.call-update) | async-done | bytes 196624 | tf_op jit(solution)/shard_map/psum | solution.py:53
  389.5 4.5 fusion.4
  394.0 2.0 fusion.28
  396.8 31.5 %all-reduce.31.cloned.1.call-done = f32[32,1536]{1,0:T(8,128)} async-done(((f32[32,1536]{1,0:T(8,128)}), f32[32,1536]{1,0:T(8,128)}) %all-reduce.31.cloned.1.call-update) | async-done | bytes 196624 | tf_op jit(solution)/shard_map/psum | solution.py:67
  430.0 3.4 fusion.2
  436.2 34.9 %all-reduce.33.cloned.1.call-done = f32[32,1536]{1,0:T(8,128)} async-done(((f32[32,1536]{1,0:T(8,128)}), f32[32,1536]{1,0:T(8,128)}) %all-reduce.33.cloned.1.call-update) | async-done | bytes 196624 | tf_op jit(solution)/shard_map/psum | solution.py:53
  473.6 4.5 fusion
  478.0 2.0 fusion.24
  480.8 31.5 %all-reduce.35.cloned.1.call-done = f32[32,1536]{1,0:T(8,128)} async-done(((f32[32,1536]{1,0:T(8,128)}), f32[32,1536]{1,0:T(8,128)}) %all-reduce.35.cloned.1.call-update) | async-done | bytes 196624 | tf_op jit(solution)/shard_map/psum | solution.py:67
  (101 shorter events, 42.2 us)
Async XLA Ops:
  7.2 46.9 %all-reduce.13.cloned.1.call-start = ((), (), s32[]{:S(2)}) async-start(), calls=%async_computation | async-start | bytes 393216 | tf_op jit(solution)/shard_map/psum | solution.py:53
  10.2 3.4 copy-start.11
  13.6 40.4 %copy-start.2 = (f32[32,1536]{1,0:T(8,128)S(1)}, f32[32,1536]{1,0:T(8,128)}, u32[]{:S(2)}) copy-start(f32[32,1536]{1,0:T(8,128)} %param.16) | copy-start | bytes 589828
  13.7 40.4 %copy-start.9 = (f32[1536]{0:T(1024)S(1)}, f32[1536]{0:T(1024)}, u32[]{:S(2)}) copy-start(f32[1536]{0:T(1024)} %param.14) | copy-start | bytes 18436
  13.7 40.4 %copy-start.10 = (f32[1536]{0:T(1024)S(1)}, f32[1536]{0:T(1024)}, u32[]{:S(2)}) copy-start(f32[1536]{0:T(1024)} %param.13) | copy-start | bytes 18436
  16.4 78.2 %all-reduce.15.cloned.1.call-start = ((), (), s32[]{:S(2)}) async-start(), calls=%async_computation.1 | async-start | bytes 393216 | tf_op jit(solution)/shard_map/psum | solution.py:67
  55.8 4.5 copy-start.12
  60.3 34.3 %copy-start = (f32[32,1536]{1,0:T(8,128)S(1)}, f32[32,1536]{1,0:T(8,128)}, u32[]{:S(2)}) copy-start(f32[32,1536]{1,0:T(8,128)} %param.15) | copy-start | bytes 589828
  60.3 34.3 %copy-start.1 = (f32[32,1536]{1,0:T(8,128)S(1)}, f32[32,1536]{1,0:T(8,128)}, u32[]{:S(2)}) copy-start(f32[32,1536]{1,0:T(8,128)} %param.17) | copy-start | bytes 589828
  63.1 74.4 %all-reduce.17.cloned.1.call-start = ((), (), s32[]{:S(2)}) async-start(), calls=%async_computation.2 | async-start | bytes 393216 | tf_op jit(solution)/shard_map/psum | solution.py:53
  99.7 37.7 %copy-start.4 = (f32[32,1536]{1,0:T(8,128)S(1)}, f32[32,1536]{1,0:T(8,128)}, u32[]{:S(2)}) copy-start(f32[32,1536]{1,0:T(8,128)} %all-reduce.13.cloned.1.call-done) | copy-start | bytes 589828
  102.5 75.6 %all-reduce.19.cloned.1.call-start = ((), (), s32[]{:S(2)}) async-start(), calls=%async_computation.3 | async-start | bytes 393216 | tf_op jit(solution)/shard_map/psum | solution.py:67
  143.7 34.3 %copy-start.8 = (f32[32,1536]{1,0:T(8,128)S(1)}, f32[32,1536]{1,0:T(8,128)}, u32[]{:S(2)}) copy-start(f32[32,1536]{1,0:T(8,128)} %all-reduce.15.cloned.1.call-done) | copy-start | bytes 589828
  146.5 74.4 %all-reduce.21.cloned.1.call-start = ((), (), s32[]{:S(2)}) async-start(), calls=%async_computation.4 | async-start | bytes 393216 | tf_op jit(solution)/shard_map/psum | solution.py:53
  185.9 75.5 %all-reduce.23.cloned.1.call-start = ((), (), s32[]{:S(2)}) async-start(), calls=%async_computation.5 | async-start | bytes 393216 | tf_op jit(solution)/shard_map/psum | solution.py:67
  229.9 74.4 %all-reduce.25.cloned.1.call-start = ((), (), s32[]{:S(2)}) async-start(), calls=%async_computation.6 | async-start | bytes 393216 | tf_op jit(solution)/shard_map/psum | solution.py:53
  266.5 37.7 %copy-start.5 = (f32[32,1536]{1,0:T(8,128)S(1)}, f32[32,1536]{1,0:T(8,128)}, u32[]{:S(2)}) copy-start(f32[32,1536]{1,0:T(8,128)} %all-reduce.21.cloned.1.call-done) | copy-start | bytes 589828
  269.3 75.6 %all-reduce.27.cloned.1.call-start = ((), (), s32[]{:S(2)}) async-start(), calls=%async_computation.7 | async-start | bytes 393216 | tf_op jit(solution)/shard_map/psum | solution.py:67
  310.6 34.3 %copy-start.6 = (f32[32,1536]{1,0:T(8,128)S(1)}, f32[32,1536]{1,0:T(8,128)}, u32[]{:S(2)}) copy-start(f32[32,1536]{1,0:T(8,128)} %all-reduce.23.cloned.1.call-done) | copy-start | bytes 589828
  313.3 74.4 %all-reduce.29.cloned.1.call-start = ((), (), s32[]{:S(2)}) async-start(), calls=%async_computation.8 | async-start | bytes 393216 | tf_op jit(solution)/shard_map/psum | solution.py:53
  352.8 75.5 %all-reduce.31.cloned.1.call-start = ((), (), s32[]{:S(2)}) async-start(), calls=%async_computation.9 | async-start | bytes 393216 | tf_op jit(solution)/shard_map/psum | solution.py:67
  396.7 74.4 %all-reduce.33.cloned.1.call-start = ((), (), s32[]{:S(2)}) async-start(), calls=%async_computation.10 | async-start | bytes 393216 | tf_op jit(solution)/shard_map/psum | solution.py:53
  433.4 37.7 %copy-start.3 = (f32[32,1536]{1,0:T(8,128)S(1)}, f32[32,1536]{1,0:T(8,128)}, u32[]{:S(2)}) copy-start(f32[32,1536]{1,0:T(8,128)} %all-reduce.29.cloned.1.call-done) | copy-start | bytes 589828
  436.1 76.2 %all-reduce.35.cloned.1.call-start = ((), (), s32[]{:S(2)}) async-start(), calls=%async_computation.11 | async-start | bytes 393216 | tf_op jit(solution)/shard_map/psum | solution.py:67
  478.0 34.3 %copy-start.7 = (f32[32,1536]{1,0:T(8,128)S(1)}, f32[32,1536]{1,0:T(8,128)}, u32[]{:S(2)}) copy-start(f32[32,1536]{1,0:T(8,128)} %all-reduce.31.cloned.1.call-done) | copy-start | bytes 589828
Sparse Core Ops, SparseCore 0:
  16.5 37.4 all-reduce.12
  63.2 31.3 all-reduce.14
  102.6 34.8 all-reduce.16
  146.6 31.3 all-reduce.18
  186.1 34.8 all-reduce.20
  230.0 31.3 all-reduce.22
  269.4 34.8 all-reduce.24
  313.4 31.3 all-reduce.26
  352.9 34.8 all-reduce.28
  396.8 31.3 all-reduce.30
  436.2 34.8 all-reduce.32
  480.9 31.3 all-reduce.34
where the time goes:
time: 530 us; the launch traced here: 521 us
  waiting for transfers between devices  401 us (76%)
  matrix products  70.8 us (13%)
  local copies, waits for them, and re-layouts  18.2 us (3%)
  between operations  15.5 us (3%)
  other arithmetic  14.8 us (3%)
    psum x6, waiting for transfers between devices, per_device(): adjoint = lax.psum(partial_adj, 'row')  212 us
    psum x6, waiting for transfers between devices, per_device(): forward = lax.psum(partial_fwd, 'col')  189 us
    dot_general x6, matrix products, per_device(): jnp.einsum('stk,tbk->stb', selected, local_tiles, preferred_element_type=...  26.8 us
    dot_general x6, matrix products, per_device(): jnp.einsum('stb,tbk->stk', adjoint_selected, local_tiles, preferred_eleme...  20.4 us
    dot_general x6, matrix products, per_device(): jnp.einsum('stb,tj->sjb', product, onehot_row, precision=lax.Precision.HI...  11.9 us
    dot_general x6, matrix products, per_device(): jnp.einsum('stk,tj->sjk', adjoint_product, onehot_col, precision=lax.Prec...  11.8 us
  transfers between devices with their start and end apart: 12, of which 12 were waited for; matrix products, arithmetic and copies ran while one was open for 0% of the time, Pallas kernels for 0%

commit v1 on v0

v1 whole, which is shorter than its diff:
```python
import functools

import jax
import jax.numpy as jnp
from jax import lax
from jax.experimental import pallas as pl
from jax.experimental.pallas import tpu as pltpu
from jax.sharding import PartitionSpec as P

ITERS = 6


PRIMAL_STEP = 0.5
DUAL_STEP = 0.2

TILE_STEP = 16
MESH = pl.DeviceIdType.MESH


def build_kernel(step_slots, rows_ref, cols_ref, count_ref, tiles_ref, k_ref, kt_ref):
    block = tiles_ref.shape[1]
    k_per = k_ref.shape[2] // block
    kt_per = kt_ref.shape[2] // block
    step = pl.program_id(0)

    @pl.when(step == 0)
    def _():
        k_ref[...] = jnp.zeros_like(k_ref)
        kt_ref[...] = jnp.zeros_like(kt_ref)

    for i in range(step_slots):
        slot = step * step_slots + i

        @pl.when(slot < count_ref[0])
        def _():
            row = rows_ref[slot]
            col = cols_ref[slot]
            tile = tiles_ref[i]
            row_at = pl.multiple_of(row * block, block)
            col_at = pl.multiple_of(col * block, block)
            k_in = pl.multiple_of(lax.rem(col, k_per) * block, block)
            kt_in = pl.multiple_of(lax.rem(row, kt_per) * block, block)
            k_ref[lax.div(col, k_per), pl.ds(row_at, block), pl.ds(k_in, block)] = tile
            kt_ref[lax.div(row, kt_per), pl.ds(col_at, block), pl.ds(kt_in, block)] = tile.T


def build_dense(tiles, rows, cols, count, cons, nvar, k_chunks, kt_chunks):
    slots, block = tiles.shape[0], tiles.shape[1]
    step_slots = TILE_STEP if slots % TILE_STEP == 0 else 1
    k_shape = (k_chunks, cons, nvar // k_chunks)
    kt_shape = (kt_chunks, nvar, cons // kt_chunks)
    return pl.pallas_call(
        functools.partial(build_kernel, step_slots),
        out_shape=(
            jax.ShapeDtypeStruct(k_shape, tiles.dtype),
            jax.ShapeDtypeStruct(kt_shape, tiles.dtype),
        ),
        grid_spec=pltpu.PrefetchScalarGridSpec(
            num_scalar_prefetch=3,
            grid=(slots // step_slots,),
            in_specs=[pl.BlockSpec((step_slots, block, block), lambda t, *_: (t, 0, 0))],
            out_specs=(
                pl.BlockSpec(k_shape, lambda t, *_: (0, 0, 0)),
                pl.BlockSpec(kt_shape, lambda t, *_: (0, 0, 0)),
            ),
        ),
        compiler_params=pltpu.CompilerParams(vmem_limit_bytes=40 << 20),
        name="build_dense",
    )(rows, cols, count, tiles)


def pdhg_kernel(
    iters,
    k_ref,
    kt_ref,
    obj_ref,
    ub_ref,
    caps_ref,
    p0_ref,
    d0_ref,
    p_out,
    d_out,
    primal,
    primal_new,
    dual,
    adj_part,
    adj_got,
    fwd_part,
    fwd_got,
    extrap_low,
    dual_low,
    adj_send,
    adj_recv,
    pri_send,
    pri_recv,
    fwd_send,
    fwd_recv,
    dua_send,
    dua_recv,
):
    halves, n_row, rows_half, v_chunk = primal.shape
    _, n_col, _, c_chunk = dual.shape
    r = lax.axis_index("row")
    c = lax.axis_index("col")

    barrier = pltpu.get_barrier_semaphore()
    for k in range(1, n_row):
        pl.semaphore_signal(
            barrier, inc=1, device_id={"row": lax.rem(r + k, n_row)}, device_id_type=MESH
        )
    for k in range(1, n_col):
        pl.semaphore_signal(
            barrier, inc=1, device_id={"col": lax.rem(c + k, n_col)}, device_id_type=MESH
        )

    v_own = pl.ds(pl.multiple_of(r * v_chunk, 128), v_chunk)
    c_own = pl.ds(pl.multiple_of(c * c_chunk, 128), c_chunk)

    def rows_of(h):
        return pl.ds(h * rows_half, rows_half)

    for h in range(halves):
        for j in range(n_row):
            primal[h, j] = p0_ref[rows_of(h), pl.ds(j * v_chunk, v_chunk)]
        for j in range(n_col):
            dual[h, j] = d0_ref[rows_of(h), pl.ds(j * c_chunk, c_chunk)]

    def spread(axis, me, count, k, src, dst, send, recv):
        return pltpu.make_async_remote_copy(
            src_ref=src,
            dst_ref=dst,
            send_sem=send,
            recv_sem=recv,
            device_id={axis: lax.rem(me + k, count)},
            device_id_type=MESH,
        )

    def adj_copy(h, k):
        dest = lax.rem(r + k, n_row)
        return spread(
            "row", r, n_row, k, adj_part.at[h, dest], adj_got.at[h, k],
            adj_send.at[h, k], adj_recv.at[h, k],
        )

    def pri_copy(h, k):
        return spread(
            "row", r, n_row, k, primal_new.at[h, r], primal_new.at[h, r],
            pri_send.at[h, k], pri_recv.at[h, k],
        )

    def fwd_copy(h, k):
        dest = lax.rem(c + k, n_col)
        return spread(
            "col", c, n_col, k, fwd_part.at[h, dest], fwd_got.at[h, k],
            fwd_send.at[h, k], fwd_recv.at[h, k],
        )

    def dua_copy(h, k):
        return spread(
            "col", c, n_col, k, dual.at[h, c], dual.at[h, c],
            dua_send.at[h, k], dua_recv.at[h, k],
        )

    def adjoint_start(h, first):
        if not first:
            for k in range(1, n_col):
                dua_copy(h, k).wait()
        for j in range(n_col):
            dual_low[h, :, j * c_chunk : (j + 1) * c_chunk] = dual[h, j].astype(jnp.bfloat16)
        for k in list(range(1, n_row)) + [0]:
            dest = lax.rem(r + k, n_row)
            adj_part[h, dest] = jnp.dot(
                dual_low[h], k_ref[dest], preferred_element_type=jnp.float32
            )
            if k:
                adj_copy(h, k).start()

    def primal_step(h):
        adjoint = adj_part[h, r]
        for k in range(1, n_row):
            adj_copy(h, k).wait()
            adjoint = adjoint + adj_got[h, k]
        primal_new[h, r] = jnp.minimum(
            jnp.maximum(primal[h, r] - PRIMAL_STEP * (obj_ref[:, v_own] - adjoint), 0.0),
            ub_ref[:, v_own],
        )
        for k in range(1, n_row):
            pri_copy(h, k).start()

    def forward_start(h):
        for k in range(1, n_row):
            pri_copy(h, k).wait()
        for j in range(n_row):
            new = primal_new[h, j]
            extrap_low[h, :, j * v_chunk : (j + 1) * v_chunk] = (
                2.0 * new - primal[h, j]
            ).astype(jnp.bfloat16)
            primal[h, j] = new
        for k in list(range(1, n_col)) + [0]:
            dest = lax.rem(c + k, n_col)
            fwd_part[h, dest] = jnp.dot(
                extrap_low[h], kt_ref[dest], preferred_element_type=jnp.float32
            )
            if k:
                fwd_copy(h, k).start()

    def dual_step(h):
        forward = fwd_part[h, c]
        for k in range(1, n_col):
            fwd_copy(h, k).wait()
            forward = forward + fwd_got[h, k]
        dual[h, c] = jnp.maximum(
            dual[h, c] + DUAL_STEP * (caps_ref[rows_of(h), c_own] - forward), 0.0
        )
        for k in range(1, n_col):
            dua_copy(h, k).start()

    pl.semaphore_wait(barrier, n_row + n_col - 2)

    if halves == 1:
        adjoint_start(0, True)
        primal_step(0)
        forward_start(0)
        dual_step(0)

        def body(_, carry):
            adjoint_start(0, False)
            primal_step(0)
            forward_start(0)
            dual_step(0)
            return carry

        lax.fori_loop(1, iters, body, 0)
    else:
        adjoint_start(0, True)
        primal_step(0)
        adjoint_start(1, True)
        forward_start(0)
        primal_step(1)
        dual_step(0)

        def body(_, carry):
            adjoint_start(0, False)
            forward_start(1)
            primal_step(0)
            dual_step(1)
            adjoint_start(1, False)
            forward_start(0)
            primal_step(1)
            dual_step(0)
            return carry

        lax.fori_loop(1, iters, body, 0)
        forward_start(1)
        dual_step(1)

    for h in range(halves):
        for j in range(n_row):
            p_out[rows_of(h), pl.ds(j * v_chunk, v_chunk)] = primal[h, j]
        for k in range(1, n_col):
            dua_copy(h, k).wait()
        for j in range(n_col):
            d_out[rows_of(h), pl.ds(j * c_chunk, c_chunk)] = dual[h, j]


def pdhg(dense, dense_t, objective, upper_bound, power_caps, primal_start, dual_start):
    n_row, cons, v_chunk = dense.shape
    n_col, nvar, c_chunk = dense_t.shape
    scenarios = primal_start.shape[0]
    halves = 2 if scenarios % 32 == 0 else 1
    rows_half = scenarios // halves
    vmem = pl.BlockSpec(memory_space=pltpu.VMEM)
    f32 = jnp.float32
    row_shape = (halves, n_row, rows_half, v_chunk)
    col_shape = (halves, n_col, rows_half, c_chunk)
    row_sem = pltpu.SemaphoreType.DMA((halves, n_row))
    col_sem = pltpu.SemaphoreType.DMA((halves, n_col))
    return pl.pallas_call(
        functools.partial(pdhg_kernel, ITERS),
        out_shape=(
            jax.ShapeDtypeStruct((scenarios, nvar), f32),
            jax.ShapeDtypeStruct((scenarios, cons), f32),
        ),
        in_specs=[vmem] * 7,
        out_specs=(vmem, vmem),
        scratch_shapes=[
            pltpu.VMEM(row_shape, f32),
            pltpu.VMEM(row_shape, f32),
            pltpu.VMEM(col_shape, f32),
            pltpu.VMEM(row_shape, f32),
            pltpu.VMEM(row_shape, f32),
            pltpu.VMEM(col_shape, f32),
            pltpu.VMEM(col_shape, f32),
            pltpu.VMEM((halves, rows_half, nvar), jnp.bfloat16),
            pltpu.VMEM((halves, rows_half, cons), jnp.bfloat16),
            row_sem,
            row_sem,
            row_sem,
            row_sem,
            col_sem,
            col_sem,
            col_sem,
            col_sem,
        ],
        compiler_params=pltpu.CompilerParams(
            collective_id=0, has_side_effects=True, vmem_limit_bytes=40 << 20
        ),
        name="pdhg",
    )(
        dense,
        dense_t,
        objective[None, :],
        upper_bound[None, :],
        power_caps,
        primal_start,
        dual_start,
    )


def pdhg_summed(dense, dense_t, objective, upper_bound, power_caps, primal, dual):
    for _ in range(ITERS):
        part = jnp.dot(dual.astype(jnp.bfloat16), dense[0], preferred_element_type=jnp.float32)
        adjoint = lax.psum(part, "row")
        new = jnp.minimum(
            jnp.maximum(primal - PRIMAL_STEP * (objective[None, :] - adjoint), 0.0),
            upper_bound[None, :],
        )
        extrap = (2.0 * new - primal).astype(jnp.bfloat16)
        part = jnp.dot(extrap, dense_t[0], preferred_element_type=jnp.float32)
        forward = lax.psum(part, "col")
        dual = jnp.maximum(dual + DUAL_STEP * (power_caps - forward), 0.0)
        primal = new
    return primal, dual


def per_device(
    n_row,
    n_col,
    block_tiles,
    tile_row,
    tile_col,
    tile_count,
    objective,
    upper_bound,
    power_caps,
    primal_start,
    dual_start,
):
    block = block_tiles.shape[-1]
    cons = dual_start.shape[1]
    nvar = primal_start.shape[1]
    even = (nvar // block) % n_row == 0 and (cons // block) % n_col == 0
    dense, dense_t = build_dense(
        block_tiles[0, 0],
        tile_row[0, 0],
        tile_col[0, 0],
        tile_count[0],
        cons,
        nvar,
        n_row if even else 1,
        n_col if even else 1,
    )
    steps = pdhg if even else pdhg_summed
    return steps(dense, dense_t, objective, upper_bound, power_caps, primal_start, dual_start)


def solution(mesh):
    return jax.shard_map(
        functools.partial(per_device, mesh.shape["row"], mesh.shape["col"]),
        mesh=mesh,
        in_specs=(
            P(("groups", "row"), "col", None, None, None),
            P(("groups", "row"), "col", None),
            P(("groups", "row"), "col", None),
            P(("groups", "row"), "col"),
            P(("groups", "col")),
            P(("groups", "col")),
            P("groups", "row"),
            P("groups", "col"),
            P("groups", "row"),
        ),
        out_specs=(P("groups", "col"), P("groups", "row")),
        check_vma=False,
    )
```

time: 530 us -> 124 us (0.23); the launches traced: 521 us -> 124 us
  waiting for transfers between devices: 401 us -> 0 us
  Pallas kernels: 0 us -> 113 us
  matrix products: 70.8 us -> 0 us
  other arithmetic: 14.8 us -> 0 us
  between operations: 15.5 us -> 1.31 us
  local copies, waits for them, and re-layouts: 18.2 us -> 9.03 us
    psum x12 -> x0, waiting for transfers between devices: 401 us -> none  [the longest x6 212 us: per_device(): adjoint = lax.psum(partial_adj, 'row')]
    pallas_call x0 -> x2, Pallas kernels: none -> 113 us  [the longest x1 109 us: pdhg(): pl.pallas_call(functools.partial(pdhg_kernel, ITERS), out_shape=(jax.Shap...]
    dot_general x24 -> x0, matrix products: 70.8 us -> none  [the longest x6 26.8 us: per_device(): jnp.einsum('stk,tbk->stb', selected, local_tiles, preferred_element_type=...]
    gather x12 -> x0, local copies, waits for them, and re-layouts: 9.11 us -> none  [the longest x6 4.56 us: per_device(): selected = primal_three[:, local_cols]]
    reshape x7 -> x0, other arithmetic: 6.79 us -> none  [the longest x4 3.84 us: per_device(): dual_three = dual_low.reshape(scenarios, row_blocks, block_size)]
    unnamed x5 -> x0, other arithmetic: 5.71 us -> none
  transfers between devices with their start and end apart: 12 -> 0, of which waited for: 12 -> 0; matrix products, arithmetic and copies ran while one was open for 0% -> 0% of each run, Pallas kernels for 0% -> 0%
where the time goes in v1:
time: 124 us
  Pallas kernels  113 us (91%)
  local copies, waits for them, and re-layouts  9.03 us (7%)
  between operations  1.31 us (1%)
    pallas_call x1, Pallas kernels, pdhg(): pl.pallas_call(functools.partial(pdhg_kernel, ITERS), out_shape=(jax.Shap...  109 us
    unnamed x14, local copies, waits for them, and re-layouts  7.63 us
    pallas_call x1, Pallas kernels, build_dense(): pl.pallas_call(functools.partial(build_kernel, step_slots), out_shape=(ja...  4.44 us

profile of v1, /device:TPU:0, one launch (start us, length us, event | category | flops | bytes accessed | tf_op | source)
XLA Modules:
  0.0 123.8 jit_solution(15511593433764632080)
XLA Ops:
  1.3 0.7 broadcast_in_dim.6.obj_ref
  2.0 0.7 broadcast_in_dim.7.ub_ref
  2.7 0.0 copy-start
  2.7 2.2 %copy-done = bf16[1,1,128,128,128]{4,3,2,1,0:T(8,128)(2,1)S(1)} copy-done((bf16[1,1,128,128,128]{4,3,2,1,0:T(8,128)(2,1)S(1)}, bf16[1,1,128,128,128]{4,3,2,1,0:T(8,128)(2,1)}, u32[]{:S(2)}) %copy-start) | copy-done | bytes 4194328
  4.9 0.0 copy-start.4
  4.9 0.7 copy-done.4
  5.5 0.0 copy-start.5
  5.5 0.7 copy-done.5
  6.2 4.4 %build_dense.1 = (bf16[4,1536,384]{2,1,0:T(8,128)(2,1)S(1)}, bf16[4,1536,384]{2,1,0:T(8,128)(2,1)S(1)}) custom-call(s32[128]{0:T(128)S(1)} %bitcast.6, s32[128]{0:T(128)S(1)} %bitcast.7, s32[1]{0:T(128)} %bitcast.4.count_ref, bf16[128,128,128]{2,1,0:T(8,128)(2,1)S(1)} %bitcast.5), custom_call_target="tpu_custom_call" | custom-call | tf_op jit(solution)/shard_map/build_dense/pallas_call | solution.py:52
  10.6 0.0 copy-start.1
  10.6 0.9 copy-done.1
  11.6 0.0 copy-start.2
  11.6 0.9 copy-done.2
  12.5 0.0 copy-start.3
  12.5 0.9 copy-done.3
  13.4 109.0 %pdhg.1 = (f32[32,1536]{1,0:T(8,128)S(1)}, f32[32,1536]{1,0:T(8,128)S(1)}) custom-call(bf16[4,1536,384]{2,1,0:T(8,128)(2,1)S(1)} %get-tuple-element.4.k_ref, bf16[4,1536,384]{2,1,0:T(8,128)(2,1)S(1)} %get-tuple-element.5.kt_ref, f32[1,1536]{1,0:T(1,128)S(1)} %broadcast_in_dim.6.obj_ref, f32[1,1536]{1,0:T(1,128)S(1)} %broadcast_in_dim.7.ub_ref, ...), custom_call_target="tpu_custom_call" | custom-call | tf_op jit(solution)/shard_map/pdhg/pallas_call | solution.py:278
  122.5 0.7 copy.14
  123.1 0.7 copy.15
Async XLA Ops:
  2.7 2.2 %copy-start = (bf16[1,1,128,128,128]{4,3,2,1,0:T(8,128)(2,1)S(1)}, bf16[1,1,128,128,128]{4,3,2,1,0:T(8,128)(2,1)}, u32[]{:S(2)}) copy-start(bf16[1,1,128,128,128]{4,3,2,1,0:T(8,128)(2,1)} %param.9) | copy-start | bytes 12582916
  4.9 0.7 copy-start.4
  5.5 0.7 copy-start.5
  10.6 0.9 copy-start.1
  11.6 0.9 copy-start.2
  12.5 0.9 copy-start.3

commit v2 on v0

v2 whole, which is shorter than its diff:
```python
import functools

import jax
import jax.numpy as jnp
from jax import lax
from jax.experimental import pallas as pl
from jax.experimental.pallas import tpu as pltpu
from jax.sharding import PartitionSpec as P

ITERS = 6


PRIMAL_STEP = 0.5
DUAL_STEP = 0.2

TILE_STEP = 16
GROUPS = 2
PIECES = 2
MESH = pl.DeviceIdType.MESH


def build_kernel(step_slots, rows_ref, cols_ref, count_ref, tiles_ref, k_ref):
    block = tiles_ref.shape[1]
    step = pl.program_id(0)

    @pl.when(step == 0)
    def _():
        k_ref[...] = jnp.zeros_like(k_ref)

    for i in range(step_slots):
        slot = step * step_slots + i

        @pl.when(slot < count_ref[0])
        def _():
            row_at = pl.multiple_of(rows_ref[slot] * block, block)
            col_at = pl.multiple_of(cols_ref[slot] * block, block)
            k_ref[pl.ds(row_at, block), pl.ds(col_at, block)] = tiles_ref[i]


def build_dense(tiles, rows, cols, count, cons, nvar):
    slots, block = tiles.shape[0], tiles.shape[1]
    step_slots = TILE_STEP if slots % TILE_STEP == 0 else 1
    return pl.pallas_call(
        functools.partial(build_kernel, step_slots),
        out_shape=jax.ShapeDtypeStruct((cons, nvar), tiles.dtype),
        grid_spec=pltpu.PrefetchScalarGridSpec(
            num_scalar_prefetch=3,
            grid=(slots // step_slots,),
            in_specs=[pl.BlockSpec((step_slots, block, block), lambda t, *_: (t, 0, 0))],
            out_specs=pl.BlockSpec((cons, nvar), lambda t, *_: (0, 0)),
        ),
        compiler_params=pltpu.CompilerParams(vmem_limit_bytes=40 << 20),
        name="build_dense",
    )(rows, cols, count, tiles)


def partner(me, stage):
    low = 1 << stage
    bit = lax.rem(lax.div(me, low), 2)
    return me + low - 2 * low * bit


def pdhg_kernel(
    iters,
    block,
    k_ref,
    obj_ref,
    ub_ref,
    caps_ref,
    p0_ref,
    d0_ref,
    primal,
    dual,
    kt_ref,
    adj_sum,
    adj_got,
    fwd_sum,
    fwd_got,
    adj_send,
    adj_recv,
    fwd_send,
    fwd_recv,
):
    row_stages, groups, pieces, rows, v_piece = adj_sum.shape
    col_stages, _, _, _, c_piece = fwd_sum.shape
    cons, nvar = k_ref.shape
    r = lax.axis_index("row")
    c = lax.axis_index("col")

    barrier = pltpu.get_barrier_semaphore()
    for s in range(row_stages):
        pl.semaphore_signal(
            barrier, inc=1, device_id={"row": partner(r, s)}, device_id_type=MESH
        )
    for s in range(col_stages):
        pl.semaphore_signal(
            barrier, inc=1, device_id={"col": partner(c, s)}, device_id_type=MESH
        )

    primal[...] = p0_ref[...]
    dual[...] = d0_ref[...]

    def rows_of(g):
        return pl.ds(g * rows, rows)

    def adj_copy(s, g, n, parity):
        return pltpu.make_async_remote_copy(
            src_ref=adj_sum.at[s, g, n],
            dst_ref=adj_got.at[parity, s, g, n],
            send_sem=adj_send.at[s, g, n],
            recv_sem=adj_recv.at[parity, s, g, n],
            device_id={"row": partner(r, s)},
            device_id_type=MESH,
        )

    def fwd_copy(s, g, n, parity):
        return pltpu.make_async_remote_copy(
            src_ref=fwd_sum.at[s, g, n],
            dst_ref=fwd_got.at[parity, s, g, n],
            send_sem=fwd_send.at[s, g, n],
            recv_sem=fwd_recv.at[parity, s, g, n],
            device_id={"col": partner(c, s)},
            device_id_type=MESH,
        )

    def exchange(copy, total, got, stages, parity, first, finish):
        for s in range(stages):
            for g in range(groups):
                for n in range(pieces):
                    copy(s, g, n, parity).wait_recv()
                    value = total[s, g, n] + got[parity, s, g, n]
                    if s + 1 < stages:
                        if not first:
                            copy(s + 1, g, n, parity).wait_send()
                        total[s + 1, g, n] = value
                        copy(s + 1, g, n, parity).start()
                    else:
                        finish(g, n, value)
                if s + 1 == stages:
                    finish(g, None, None)

    def products(copy, total, width, lhs, weights, g, parity, first):
        for n in range(pieces):
            if not first:
                copy(0, g, n, parity).wait_send()
            total[0, g, n] = jnp.dot(
                lhs, weights[:, n * width : (n + 1) * width], preferred_element_type=jnp.float32
            )
            copy(0, g, n, parity).start()

    def adjoint_start(g, parity, first):
        low = dual[rows_of(g), :].astype(jnp.bfloat16)
        products(adj_copy, adj_sum, v_piece, low, k_ref, g, parity, first)

    def iteration(parity, first, last):
        extrap = [[None] * pieces for _ in range(groups)]

        def primal_step(g, n, adjoint):
            if n is None:
                low = jnp.concatenate(extrap[g], axis=1)
                products(fwd_copy, fwd_sum, c_piece, low, kt_ref, g, parity, first)
                return
            lanes = pl.ds(n * v_piece, v_piece)
            old = primal[rows_of(g), lanes]
            new = jnp.minimum(
                jnp.maximum(old - PRIMAL_STEP * (obj_ref[:, lanes] - adjoint), 0.0),
                ub_ref[:, lanes],
            )
            primal[rows_of(g), lanes] = new
            extrap[g][n] = (2.0 * new - old).astype(jnp.bfloat16)

        def dual_step(g, n, forward):
            if n is None:
                if not last:
                    adjoint_start(g, 1 - parity, False)
                return
            lanes = pl.ds(n * c_piece, c_piece)
            dual[rows_of(g), lanes] = jnp.maximum(
                dual[rows_of(g), lanes]
                + DUAL_STEP * (caps_ref[rows_of(g), lanes] - forward),
                0.0,
            )

        exchange(adj_copy, adj_sum, adj_got, row_stages, parity, first, primal_step)
        exchange(fwd_copy, fwd_sum, fwd_got, col_stages, parity, first, dual_step)

    pl.semaphore_wait(barrier, row_stages + col_stages)

    for g in range(groups):
        adjoint_start(g, 0, True)

    def transpose_rows(i, carry):
        at = pl.multiple_of(i * block, block)
        for j in range(nvar // block):
            kt_ref[j * block : (j + 1) * block, pl.ds(at, block)] = k_ref[
                pl.ds(at, block), j * block : (j + 1) * block
            ].T
        return carry

    lax.fori_loop(0, cons // block, transpose_rows, 0)

    iteration(0, True, False)

    def body(i, carry):
        iteration(lax.rem(i, 2), False, False)
        return carry

    lax.fori_loop(1, iters - 1, body, 0)
    iteration((iters - 1) % 2, False, True)

    for g in range(groups):
        for n in range(pieces):
            for s in range(row_stages):
                adj_copy(s, g, n, 0).wait_send()
            for s in range(col_stages):
                fwd_copy(s, g, n, 0).wait_send()


def pdhg(block, n_row, n_col, dense, objective, upper_bound, power_caps, primal_start, dual_start):
    cons, nvar = dense.shape
    scenarios = primal_start.shape[0]
    groups, pieces = GROUPS, PIECES
    row_stages, col_stages = n_row.bit_length() - 1, n_col.bit_length() - 1
    assert (1 << row_stages, 1 << col_stages) == (n_row, n_col)
    rows = scenarios // groups
    vmem = pl.BlockSpec(memory_space=pltpu.VMEM)
    f32 = jnp.float32
    adj = (row_stages, groups, pieces)
    fwd = (col_stages, groups, pieces)
    v_piece, c_piece = nvar // pieces, cons // pieces
    return pl.pallas_call(
        functools.partial(pdhg_kernel, ITERS, block),
        out_shape=(
            jax.ShapeDtypeStruct((scenarios, nvar), f32),
            jax.ShapeDtypeStruct((scenarios, cons), f32),
        ),
        in_specs=[vmem] * 6,
        out_specs=(vmem, vmem),
        scratch_shapes=[
            pltpu.VMEM((nvar, cons), dense.dtype),
            pltpu.VMEM((*adj, rows, v_piece), f32),
            pltpu.VMEM((2, *adj, rows, v_piece), f32),
            pltpu.VMEM((*fwd, rows, c_piece), f32),
            pltpu.VMEM((2, *fwd, rows, c_piece), f32),
            pltpu.SemaphoreType.DMA(adj),
            pltpu.SemaphoreType.DMA((2, *adj)),
            pltpu.SemaphoreType.DMA(fwd),
            pltpu.SemaphoreType.DMA((2, *fwd)),
        ],
        compiler_params=pltpu.CompilerParams(
            collective_id=0, has_side_effects=True, vmem_limit_bytes=40 << 20
        ),
        name="pdhg",
    )(
        dense,
        objective[None, :],
        upper_bound[None, :],
        power_caps,
        primal_start,
        dual_start,
    )


def per_device(
    n_row,
    n_col,
    block_tiles,
    tile_row,
    tile_col,
    tile_count,
    objective,
    upper_bound,
    power_caps,
    primal_start,
    dual_start,
):
    dense = build_dense(
        block_tiles[0, 0],
        tile_row[0, 0],
        tile_col[0, 0],
        tile_count[0],
        dual_start.shape[1],
        primal_start.shape[1],
    )
    return pdhg(
        block_tiles.shape[-1],
        n_row,
        n_col,
        dense,
        objective,
        upper_bound,
        power_caps,
        primal_start,
        dual_start,
    )


def solution(mesh):
    return jax.shard_map(
        functools.partial(per_device, mesh.shape["row"], mesh.shape["col"]),
        mesh=mesh,
        in_specs=(
            P(("groups", "row"), "col", None, None, None),
            P(("groups", "row"), "col", None),
            P(("groups", "row"), "col", None),
            P(("groups", "row"), "col"),
            P(("groups", "col")),
            P(("groups", "col")),
            P("groups", "row"),
            P("groups", "col"),
            P("groups", "row"),
        ),
        out_specs=(P("groups", "col"), P("groups", "row")),
        check_vma=False,
    )
```

time: 530 us -> 129 us (0.24); the launches traced: 521 us -> 129 us
  waiting for transfers between devices: 401 us -> 0 us
  Pallas kernels: 0 us -> 121 us
  matrix products: 70.8 us -> 0 us
  other arithmetic: 14.8 us -> 0 us
  between operations: 15.5 us -> 1.32 us
  local copies, waits for them, and re-layouts: 18.2 us -> 6.27 us
    psum x12 -> x0, waiting for transfers between devices: 401 us -> none  [the longest x6 212 us: per_device(): adjoint = lax.psum(partial_adj, 'row')]
    pallas_call x0 -> x2, Pallas kernels: none -> 121 us  [the longest x1 119 us: pdhg(): pl.pallas_call(functools.partial(pdhg_kernel, ITERS, block), out_shape=(j...]
    dot_general x24 -> x0, matrix products: 70.8 us -> none  [the longest x6 26.8 us: per_device(): jnp.einsum('stk,tbk->stb', selected, local_tiles, preferred_element_type=...]
    gather x12 -> x0, local copies, waits for them, and re-layouts: 9.11 us -> none  [the longest x6 4.56 us: per_device(): selected = primal_three[:, local_cols]]
    reshape x7 -> x0, other arithmetic: 6.79 us -> none  [the longest x4 3.84 us: per_device(): dual_three = dual_low.reshape(scenarios, row_blocks, block_size)]
    unnamed x5 -> x0, other arithmetic: 5.71 us -> none
  transfers between devices with their start and end apart: 12 -> 0, of which waited for: 12 -> 0; matrix products, arithmetic and copies ran while one was open for 0% -> 0% of each run, Pallas kernels for 0% -> 0%
where the time goes in v2:
time: 129 us
  Pallas kernels  121 us (94%)
  local copies, waits for them, and re-layouts  6.27 us (5%)
  between operations  1.32 us (1%)
    pallas_call x1, Pallas kernels, pdhg(): pl.pallas_call(functools.partial(pdhg_kernel, ITERS, block), out_shape=(j...  119 us
    unnamed x14, local copies, waits for them, and re-layouts  4.86 us

profile of v2, /device:TPU:0, one launch (start us, length us, event | category | flops | bytes accessed | tf_op | source)
XLA Modules:
  0.0 128.7 jit_solution(7716204514158963887)
XLA Ops:
  1.3 0.7 broadcast_in_dim.6.obj_ref
  2.0 0.7 broadcast_in_dim.7.ub_ref
  2.7 0.0 copy-start
  2.7 2.2 %copy-done = bf16[1,1,128,128,128]{4,3,2,1,0:T(8,128)(2,1)S(1)} copy-done((bf16[1,1,128,128,128]{4,3,2,1,0:T(8,128)(2,1)S(1)}, bf16[1,1,128,128,128]{4,3,2,1,0:T(8,128)(2,1)}, u32[]{:S(2)}) %copy-start) | copy-done | bytes 4194328
  4.9 0.0 copy-start.4
  4.9 0.7 copy-done.4
  5.5 0.0 copy-start.5
  5.5 0.7 copy-done.5
  6.2 0.0 copy-start.1
  6.2 0.0 copy-start.2
  6.2 0.0 copy-start.3
  6.2 2.3 %build_dense.1.k_ref = bf16[1536,1536]{1,0:T(8,128)(2,1)S(1)} custom-call(s32[128]{0:T(128)S(1)} %bitcast.6, s32[128]{0:T(128)S(1)} %bitcast.7, s32[1]{0:T(128)} %bitcast.4.count_ref, bf16[128,128,128]{2,1,0:T(8,128)(2,1)S(1)} %bitcast.5), custom_call_target="tpu_custom_call" | custom-call | tf_op jit(solution)/shard_map/build_dense/pallas_call | solution.py:43
  8.4 0.0 copy-done.1
  8.5 0.0 copy-done.2
  8.5 0.0 copy-done.3
  8.5 118.8 %pdhg.1 = (f32[32,1536]{1,0:T(8,128)S(1)}, f32[32,1536]{1,0:T(8,128)S(1)}) custom-call(bf16[1536,1536]{1,0:T(8,128)(2,1)S(1)} %build_dense.1.k_ref, f32[1,1536]{1,0:T(1,128)S(1)} %broadcast_in_dim.6.obj_ref, f32[1,1536]{1,0:T(1,128)S(1)} %broadcast_in_dim.7.ub_ref, f32[32,1536]{1,0:T(8,128)S(1)} %copy-done.1, f32[32,1536]{1,0:T(8,128)S(1)} %copy-done.2, ...), custom_call_target="tpu_custom_call" | custom-call | tf_op jit(solution)/shard_map/pdhg/pallas_call | solution.py:231
  127.3 0.7 copy.14
  128.0 0.7 copy.15
Async XLA Ops:
  2.7 2.2 %copy-start = (bf16[1,1,128,128,128]{4,3,2,1,0:T(8,128)(2,1)S(1)}, bf16[1,1,128,128,128]{4,3,2,1,0:T(8,128)(2,1)}, u32[]{:S(2)}) copy-start(bf16[1,1,128,128,128]{4,3,2,1,0:T(8,128)(2,1)} %param.9) | copy-start | bytes 12582916
  4.9 0.7 copy-start.4
  5.5 0.7 copy-start.5
  6.2 2.3 %copy-start.1 = (f32[32,1536]{1,0:T(8,128)S(1)}, f32[32,1536]{1,0:T(8,128)}, u32[]{:S(2)}) copy-start(f32[32,1536]{1,0:T(8,128)} %caps_ref.1) | copy-start | bytes 589828
  6.2 2.3 %copy-start.2 = (f32[32,1536]{1,0:T(8,128)S(1)}, f32[32,1536]{1,0:T(8,128)}, u32[]{:S(2)}) copy-start(f32[32,1536]{1,0:T(8,128)} %p0_ref.1) | copy-start | bytes 589828
  6.2 2.3 %copy-start.3 = (f32[32,1536]{1,0:T(8,128)S(1)}, f32[32,1536]{1,0:T(8,128)}, u32[]{:S(2)}) copy-start(f32[32,1536]{1,0:T(8,128)} %d0_ref.1) | copy-start | bytes 589828

commit v3 on v1

--- a/solution.py
+++ b/solution.py
@@ -17,16 +17,14 @@
 MESH = pl.DeviceIdType.MESH
 
 
-def build_kernel(step_slots, rows_ref, cols_ref, count_ref, tiles_ref, k_ref, kt_ref):
+def build_kernel(step_slots, rows_ref, cols_ref, count_ref, tiles_ref, k_ref):
     block = tiles_ref.shape[1]
     k_per = k_ref.shape[2] // block
-    kt_per = kt_ref.shape[2] // block
     step = pl.program_id(0)
 
     @pl.when(step == 0)
     def _():
         k_ref[...] = jnp.zeros_like(k_ref)
-        kt_ref[...] = jnp.zeros_like(kt_ref)
 
     for i in range(step_slots):
         slot = step * step_slots + i
@@ -35,34 +33,23 @@
         def _():
             row = rows_ref[slot]
             col = cols_ref[slot]
-            tile = tiles_ref[i]
             row_at = pl.multiple_of(row * block, block)
-            col_at = pl.multiple_of(col * block, block)
             k_in = pl.multiple_of(lax.rem(col, k_per) * block, block)
-            kt_in = pl.multiple_of(lax.rem(row, kt_per) * block, block)
-            k_ref[lax.div(col, k_per), pl.ds(row_at, block), pl.ds(k_in, block)] = tile
-            kt_ref[lax.div(row, kt_per), pl.ds(col_at, block), pl.ds(kt_in, block)] = tile.T
-
-
-def build_dense(tiles, rows, cols, count, cons, nvar, k_chunks, kt_chunks):
+            k_ref[lax.div(col, k_per), pl.ds(row_at, block), pl.ds(k_in, block)] = tiles_ref[i]
+
+
+def build_dense(tiles, rows, cols, count, cons, nvar, k_chunks):
     slots, block = tiles.shape[0], tiles.shape[1]
     step_slots = TILE_STEP if slots % TILE_STEP == 0 else 1
     k_shape = (k_chunks, cons, nvar // k_chunks)
-    kt_shape = (kt_chunks, nvar, cons // kt_chunks)
     return pl.pallas_call(
         functools.partial(build_kernel, step_slots),
-        out_shape=(
-            jax.ShapeDtypeStruct(k_shape, tiles.dtype),
-            jax.ShapeDtypeStruct(kt_shape, tiles.dtype),
-        ),
+        out_shape=jax.ShapeDtypeStruct(k_shape, tiles.dtype),
         grid_spec=pltpu.PrefetchScalarGridSpec(
             num_scalar_prefetch=3,
             grid=(slots // step_slots,),
             in_specs=[pl.BlockSpec((step_slots, block, block), lambda t, *_: (t, 0, 0))],
-            out_specs=(
-                pl.BlockSpec(k_shape, lambda t, *_: (0, 0, 0)),
-                pl.BlockSpec(kt_shape, lambda t, *_: (0, 0, 0)),
-            ),
+            out_specs=pl.BlockSpec(k_shape, lambda t, *_: (0, 0, 0)),
         ),
         compiler_params=pltpu.CompilerParams(vmem_limit_bytes=40 << 20),
         name="build_dense",
@@ -71,8 +58,8 @@
 
 def pdhg_kernel(
     iters,
+    block,
     k_ref,
-    kt_ref,
     obj_ref,
     ub_ref,
     caps_ref,
@@ -80,6 +67,7 @@
     d0_ref,
     p_out,
     d_out,
+    kt_ref,
     primal,
     primal_new,
     dual,
@@ -215,10 +203,27 @@
         for k in range(1, n_col):
             dua_copy(h, k).start()
 
+    row_blocks = c_chunk * n_col // block
+    k_per, kt_per = v_chunk // block, c_chunk // block
+
+    def transpose_rows(first, last):
+        def one(i, carry):
+            at = pl.multiple_of(i * block, block)
+            into = pl.multiple_of(lax.rem(i, kt_per) * block, block)
+            for j in range(n_row * k_per):
+                inside = j % k_per * block
+                kt_ref[lax.div(i, kt_per), j * block : (j + 1) * block, pl.ds(into, block)] = (
+                    k_ref[j // k_per, pl.ds(at, block), inside : inside + block].T
+                )
+            return carry
+
+        lax.fori_loop(first, last, one, 0)
+
     pl.semaphore_wait(barrier, n_row + n_col - 2)
 
     if halves == 1:
         adjoint_start(0, True)
+        transpose_rows(0, row_blocks)
         primal_step(0)
         forward_start(0)
         dual_step(0)
@@ -233,8 +238,10 @@
         lax.fori_loop(1, iters, body, 0)
     else:
         adjoint_start(0, True)
+        transpose_rows(0, row_blocks // 2)
         primal_step(0)
         adjoint_start(1, True)
+        transpose_rows(row_blocks // 2, row_blocks)
         forward_start(0)
         primal_step(1)
         dual_step(0)
@@ -263,9 +270,9 @@
             d_out[rows_of(h), pl.ds(j * c_chunk, c_chunk)] = dual[h, j]
 
 
-def pdhg(dense, dense_t, objective, upper_bound, power_caps, primal_start, dual_start):
+def pdhg(block, n_col, dense, objective, upper_bound, power_caps, primal_start, dual_start):
     n_row, cons, v_chunk = dense.shape
-    n_col, nvar, c_chunk = dense_t.shape
+    nvar, c_chunk = n_row * v_chunk, cons // n_col
     scenarios = primal_start.shape[0]
     halves = 2 if scenarios % 32 == 0 else 1
     rows_half = scenarios // halves
@@ -276,14 +283,15 @@
     row_sem = pltpu.SemaphoreType.DMA((halves, n_row))
     col_sem = pltpu.SemaphoreType.DMA((halves, n_col))
     return pl.pallas_call(
-        functools.partial(pdhg_kernel, ITERS),
+        functools.partial(pdhg_kernel, ITERS, block),
         out_shape=(
             jax.ShapeDtypeStruct((scenarios, nvar), f32),
             jax.ShapeDtypeStruct((scenarios, cons), f32),
         ),
-        in_specs=[vmem] * 7,
+        in_specs=[vmem] * 6,
         out_specs=(vmem, vmem),
         scratch_shapes=[
+            pltpu.VMEM((n_col, nvar, c_chunk), dense.dtype),
             pltpu.VMEM(row_shape, f32),
             pltpu.VMEM(row_shape, f32),
             pltpu.VMEM(col_shape, f32),
@@ -308,7 +316,6 @@
         name="pdhg",
     )(
         dense,
-        dense_t,
         objective[None, :],
         upper_bound[None, :],
         power_caps,
@@ -317,7 +324,7 @@
     )
 
 
-def pdhg_summed(dense, dense_t, objective, upper_bound, power_caps, primal, dual):
+def pdhg_summed(dense, objective, upper_bound, power_caps, primal, dual):
     for _ in range(ITERS):
         part = jnp.dot(dual.astype(jnp.bfloat16), dense[0], preferred_element_type=jnp.float32)
         adjoint = lax.psum(part, "row")
@@ -326,7 +333,7 @@
             upper_bound[None, :],
         )
         extrap = (2.0 * new - primal).astype(jnp.bfloat16)
-        part = jnp.dot(extrap, dense_t[0], preferred_element_type=jnp.float32)
+        part = jnp.dot(extrap, dense[0].T, preferred_element_type=jnp.float32)
         forward = lax.psum(part, "col")
         dual = jnp.maximum(dual + DUAL_STEP * (power_caps - forward), 0.0)
         primal = new
@@ -350,7 +357,7 @@
     cons = dual_start.shape[1]
     nvar = primal_start.shape[1]
     even = (nvar // block) % n_row == 0 and (cons // block) % n_col == 0
-    dense, dense_t = build_dense(
+    dense = build_dense(
         block_tiles[0, 0],
         tile_row[0, 0],
         tile_col[0, 0],
@@ -358,10 +365,9 @@
         cons,
         nvar,
         n_row if even else 1,
-        n_col if even else 1,
     )
-    steps = pdhg if even else pdhg_summed
-    return steps(dense, dense_t, objective, upper_bound, power_caps, primal_start, dual_start)
+    steps = functools.partial(pdhg, block, n_col) if even else pdhg_summed
+    return steps(dense, objective, upper_bound, power_caps, primal_start, dual_start)
 
 
 def solution(mesh):

time: 124 us -> 116 us (0.935)
  Pallas kernels: 113 us -> 109 us
  local copies, waits for them, and re-layouts: 9.03 us -> 6.27 us
    pallas_call x2, Pallas kernels: 113 us -> 109 us  [the longest x1 106 us: pdhg(): pl.pallas_call(functools.partial(pdhg_kernel, ITERS, block), out_shape=(j...]
    unnamed x14, local copies, waits for them, and re-layouts: 7.63 us -> 4.86 us
where the time goes in v3:
time: 116 us; the launch traced here: 117 us
  Pallas kernels  109 us (94%)
  local copies, waits for them, and re-layouts  6.27 us (5%)
  between operations  1.32 us (1%)
    pallas_call x1, Pallas kernels, pdhg(): pl.pallas_call(functools.partial(pdhg_kernel, ITERS, block), out_shape=(j...  106 us
    unnamed x14, local copies, waits for them, and re-layouts  4.86 us
    pallas_call x1, Pallas kernels, build_dense(): pl.pallas_call(functools.partial(build_kernel, step_slots), out_shape=jax...  2.64 us

profile of v3, /device:TPU:0, one launch (start us, length us, event | category | flops | bytes accessed | tf_op | source)
XLA Modules:
  0.0 116.6 jit_solution(6907698091764265089)
XLA Ops:
  1.3 0.7 broadcast_in_dim.6.obj_ref
  2.0 0.7 broadcast_in_dim.7.ub_ref
  2.7 0.0 copy-start
  2.7 2.2 %copy-done = bf16[1,1,128,128,128]{4,3,2,1,0:T(8,128)(2,1)S(1)} copy-done((bf16[1,1,128,128,128]{4,3,2,1,0:T(8,128)(2,1)S(1)}, bf16[1,1,128,128,128]{4,3,2,1,0:T(8,128)(2,1)}, u32[]{:S(2)}) %copy-start) | copy-done | bytes 4194328
  4.9 0.0 copy-start.4
  4.9 0.7 copy-done.4
  5.5 0.0 copy-start.5
  5.5 0.7 copy-done.5
  6.2 0.0 copy-start.1
  6.2 0.0 copy-start.2
  6.2 0.0 copy-start.3
  6.2 2.6 %build_dense.1.k_ref = bf16[4,1536,384]{2,1,0:T(8,128)(2,1)S(1)} custom-call(s32[128]{0:T(128)S(1)} %bitcast.6, s32[128]{0:T(128)S(1)} %bitcast.7, s32[1]{0:T(128)} %bitcast.4.count_ref, bf16[128,128,128]{2,1,0:T(8,128)(2,1)S(1)} %bitcast.5), custom_call_target="tpu_custom_call" | custom-call | tf_op jit(solution)/shard_map/build_dense/pallas_call | solution.py:45
  8.8 0.0 copy-done.1
  8.8 0.0 copy-done.2
  8.9 0.0 copy-done.3
  8.9 106.4 %pdhg.1 = (f32[32,1536]{1,0:T(8,128)S(1)}, f32[32,1536]{1,0:T(8,128)S(1)}) custom-call(bf16[4,1536,384]{2,1,0:T(8,128)(2,1)S(1)} %build_dense.1.k_ref, f32[1,1536]{1,0:T(1,128)S(1)} %broadcast_in_dim.6.obj_ref, f32[1,1536]{1,0:T(1,128)S(1)} %broadcast_in_dim.7.ub_ref, f32[32,1536]{1,0:T(8,128)S(1)} %copy-done.1, f32[32,1536]{1,0:T(8,128)S(1)} %copy-done.2, ...), custom_call_target="tpu_custom_call" | custom-call | tf_op jit(solution)/shard_map/pdhg/pallas_call | solution.py:285
  115.2 0.7 copy.14
  115.9 0.7 copy.15
Async XLA Ops:
  2.7 2.2 %copy-start = (bf16[1,1,128,128,128]{4,3,2,1,0:T(8,128)(2,1)S(1)}, bf16[1,1,128,128,128]{4,3,2,1,0:T(8,128)(2,1)}, u32[]{:S(2)}) copy-start(bf16[1,1,128,128,128]{4,3,2,1,0:T(8,128)(2,1)} %param.9) | copy-start | bytes 12582916
  4.9 0.7 copy-start.4
  5.5 0.7 copy-start.5
  6.2 2.7 %copy-start.1 = (f32[32,1536]{1,0:T(8,128)S(1)}, f32[32,1536]{1,0:T(8,128)}, u32[]{:S(2)}) copy-start(f32[32,1536]{1,0:T(8,128)} %caps_ref.1) | copy-start | bytes 589828
  6.2 2.7 %copy-start.2 = (f32[32,1536]{1,0:T(8,128)S(1)}, f32[32,1536]{1,0:T(8,128)}, u32[]{:S(2)}) copy-start(f32[32,1536]{1,0:T(8,128)} %p0_ref.1) | copy-start | bytes 589828
  6.2 2.7 %copy-start.3 = (f32[32,1536]{1,0:T(8,128)S(1)}, f32[32,1536]{1,0:T(8,128)}, u32[]{:S(2)}) copy-start(f32[32,1536]{1,0:T(8,128)} %d0_ref.1) | copy-start | bytes 589828

commit v4 on v3

--- a/solution.py
+++ b/solution.py
@@ -54,6 +54,16 @@
         compiler_params=pltpu.CompilerParams(vmem_limit_bytes=40 << 20),
         name="build_dense",
     )(rows, cols, count, tiles)
+
+
+def peer(me, k, count):
+    if count & (count - 1):
+        return lax.rem(me + k, count)
+    for bit in range(count.bit_length() - 1):
+        low = 1 << bit
+        if k & low:
+            me = me + low - 2 * low * lax.rem(lax.div(me, low), 2)
+    return me
 
 
 def pdhg_kernel(
@@ -94,11 +104,11 @@
     barrier = pltpu.get_barrier_semaphore()
     for k in range(1, n_row):
         pl.semaphore_signal(
-            barrier, inc=1, device_id={"row": lax.rem(r + k, n_row)}, device_id_type=MESH
+            barrier, inc=1, device_id={"row": peer(r, k, n_row)}, device_id_type=MESH
         )
     for k in range(1, n_col):
         pl.semaphore_signal(
-            barrier, inc=1, device_id={"col": lax.rem(c + k, n_col)}, device_id_type=MESH
+            barrier, inc=1, device_id={"col": peer(c, k, n_col)}, device_id_type=MESH
         )
 
     v_own = pl.ds(pl.multiple_of(r * v_chunk, 128), v_chunk)
@@ -119,12 +129,12 @@
             dst_ref=dst,
             send_sem=send,
             recv_sem=recv,
-            device_id={axis: lax.rem(me + k, count)},
+            device_id={axis: peer(me, k, count)},
             device_id_type=MESH,
         )
 
     def adj_copy(h, k):
-        dest = lax.rem(r + k, n_row)
+        dest = peer(r, k, n_row)
         return spread(
             "row", r, n_row, k, adj_part.at[h, dest], adj_got.at[h, k],
             adj_send.at[h, k], adj_recv.at[h, k],
@@ -137,7 +147,7 @@
         )
 
     def fwd_copy(h, k):
-        dest = lax.rem(c + k, n_col)
+        dest = peer(c, k, n_col)
         return spread(
             "col", c, n_col, k, fwd_part.at[h, dest], fwd_got.at[h, k],
             fwd_send.at[h, k], fwd_recv.at[h, k],
@@ -155,8 +165,8 @@
                 dua_copy(h, k).wait()
         for j in range(n_col):
             dual_low[h, :, j * c_chunk : (j + 1) * c_chunk] = dual[h, j].astype(jnp.bfloat16)
-        for k in list(range(1, n_row)) + [0]:
-            dest = lax.rem(r + k, n_row)
+        for k in range(n_row - 1, -1, -1):
+            dest = peer(r, k, n_row)
             adj_part[h, dest] = jnp.dot(
                 dual_low[h], k_ref[dest], preferred_element_type=jnp.float32
             )
@@ -172,7 +182,7 @@
             jnp.maximum(primal[h, r] - PRIMAL_STEP * (obj_ref[:, v_own] - adjoint), 0.0),
             ub_ref[:, v_own],
         )
-        for k in range(1, n_row):
+        for k in range(n_row - 1, 0, -1):
             pri_copy(h, k).start()
 
     def forward_start(h):
@@ -184,8 +194,8 @@
                 2.0 * new - primal[h, j]
             ).astype(jnp.bfloat16)
             primal[h, j] = new
-        for k in list(range(1, n_col)) + [0]:
-            dest = lax.rem(c + k, n_col)
+        for k in range(n_col - 1, -1, -1):
+            dest = peer(c, k, n_col)
             fwd_part[h, dest] = jnp.dot(
                 extrap_low[h], kt_ref[dest], preferred_element_type=jnp.float32
             )
@@ -200,7 +210,7 @@
         dual[h, c] = jnp.maximum(
             dual[h, c] + DUAL_STEP * (caps_ref[rows_of(h), c_own] - forward), 0.0
         )
-        for k in range(1, n_col):
+        for k in range(n_col - 1, 0, -1):
             dua_copy(h, k).start()
 
     row_blocks = c_chunk * n_col // block

time: 116 us -> 117 us (level)
  no operation moved by 1% of the time
where the time goes in v4:
time: 117 us
  Pallas kernels  109 us (93%)
  local copies, waits for them, and re-layouts  6.27 us (5%)
  between operations  1.32 us (1%)
    pallas_call x1, Pallas kernels, pdhg(): pl.pallas_call(functools.partial(pdhg_kernel, ITERS, block), out_shape=(j...  107 us
    unnamed x14, local copies, waits for them, and re-layouts  4.86 us
    pallas_call x1, Pallas kernels, build_dense(): pl.pallas_call(functools.partial(build_kernel, step_slots), out_shape=jax...  2.54 us

profile of v4, /device:TPU:0, one launch (start us, length us, event | category | flops | bytes accessed | tf_op | source)
XLA Modules:
  0.0 116.7 jit_solution(12787617228758657258)
XLA Ops:
  1.3 0.7 broadcast_in_dim.6.obj_ref
  2.0 0.7 broadcast_in_dim.7.ub_ref
  2.7 0.0 copy-start
  2.7 2.2 %copy-done = bf16[1,1,128,128,128]{4,3,2,1,0:T(8,128)(2,1)S(1)} copy-done((bf16[1,1,128,128,128]{4,3,2,1,0:T(8,128)(2,1)S(1)}, bf16[1,1,128,128,128]{4,3,2,1,0:T(8,128)(2,1)}, u32[]{:S(2)}) %copy-start) | copy-done | bytes 4194328
  4.9 0.0 copy-start.4
  4.9 0.7 copy-done.4
  5.5 0.0 copy-start.5
  5.5 0.7 copy-done.5
  6.2 0.0 copy-start.1
  6.2 0.0 copy-start.2
  6.2 0.0 copy-start.3
  6.2 2.5 %build_dense.1.k_ref = bf16[4,1536,384]{2,1,0:T(8,128)(2,1)S(1)} custom-call(s32[128]{0:T(128)S(1)} %bitcast.6, s32[128]{0:T(128)S(1)} %bitcast.7, s32[1]{0:T(128)} %bitcast.4.count_ref, bf16[128,128,128]{2,1,0:T(8,128)(2,1)S(1)} %bitcast.5), custom_call_target="tpu_custom_call" | custom-call | tf_op jit(solution)/shard_map/build_dense/pallas_call | solution.py:45
  8.7 0.0 copy-done.1
  8.7 0.0 copy-done.2
  8.8 0.0 copy-done.3
  8.8 106.5 %pdhg.1 = (f32[32,1536]{1,0:T(8,128)S(1)}, f32[32,1536]{1,0:T(8,128)S(1)}) custom-call(bf16[4,1536,384]{2,1,0:T(8,128)(2,1)S(1)} %build_dense.1.k_ref, f32[1,1536]{1,0:T(1,128)S(1)} %broadcast_in_dim.6.obj_ref, f32[1,1536]{1,0:T(1,128)S(1)} %broadcast_in_dim.7.ub_ref, f32[32,1536]{1,0:T(8,128)S(1)} %copy-done.1, f32[32,1536]{1,0:T(8,128)S(1)} %copy-done.2, ...), custom_call_target="tpu_custom_call" | custom-call | tf_op jit(solution)/shard_map/pdhg/pallas_call | solution.py:295
  115.3 0.7 copy.14
  116.0 0.7 copy.15
Async XLA Ops:
  2.7 2.2 %copy-start = (bf16[1,1,128,128,128]{4,3,2,1,0:T(8,128)(2,1)S(1)}, bf16[1,1,128,128,128]{4,3,2,1,0:T(8,128)(2,1)}, u32[]{:S(2)}) copy-start(bf16[1,1,128,128,128]{4,3,2,1,0:T(8,128)(2,1)} %param.9) | copy-start | bytes 12582916
  4.9 0.7 copy-start.4
  5.5 0.7 copy-start.5
  6.2 2.6 %copy-start.1 = (f32[32,1536]{1,0:T(8,128)S(1)}, f32[32,1536]{1,0:T(8,128)}, u32[]{:S(2)}) copy-start(f32[32,1536]{1,0:T(8,128)} %caps_ref.1) | copy-start | bytes 589828
  6.2 2.6 %copy-start.2 = (f32[32,1536]{1,0:T(8,128)S(1)}, f32[32,1536]{1,0:T(8,128)}, u32[]{:S(2)}) copy-start(f32[32,1536]{1,0:T(8,128)} %p0_ref.1) | copy-start | bytes 589828
  6.2 2.6 %copy-start.3 = (f32[32,1536]{1,0:T(8,128)S(1)}, f32[32,1536]{1,0:T(8,128)}, u32[]{:S(2)}) copy-start(f32[32,1536]{1,0:T(8,128)} %d0_ref.1) | copy-start | bytes 589828
